TPU v7x, 256 devices: a whole 4x4x8 slice. The times are simulated.
256 devices in a mesh: req: 16 (over y, x_hi, core), blk: 16 (over z, x_lo).
Axes of the slice: x: 4 (x_hi: 2, x_lo: 2; x = x_hi * 2 + x_lo), y: 4, z: 8, core: 2. Of those that a mesh axis runs over, the one named last changes fastest.
Arguments:
- tokens: bfloat16 [32, 256, 1600], P('req'), may hold values from -6 to 6
- cache_kv: bfloat16 [4, 8192, 16, 128], P(None, 'req', 'blk'), may hold values from -500 to 500
- w_qkv: bfloat16 [1600, 16, 192], P(None, 'blk'), may hold values from -0.15625 to 0.15625
- w_out: bfloat16 [16, 64, 1600], P('blk'), may hold values from -0.1875 to 0.1875
- w_fc: bfloat16 [1600, 6400], P(None, 'blk'), may hold values from -0.15625 to 0.15625
- w_proj: bfloat16 [6400, 1600], P('blk'), may hold values from -0.078125 to 0.078125
- embed_table: bfloat16 [50256, 1600], P('req', 'blk'), may hold values from -6 to 6
- group_ids: int32 [32], replicated, may hold values from 0 to 3, never falling along the last dimension, each value on 1 to 16 neighbouring positions
- cache_len: int32 [4], replicated, may hold values from 512 to 8192, as said below
- accept: int32 [2, 32, 256], P(None, 'req'), may hold values 0 or 1
- new_ids: int32 [2, 32, 256], replicated, may hold values from 0 to 50255
Outputs:
- denoised: bfloat16 [32, 256, 1600], P('req')
Inputs may be any that keep to these rules, and one draw needn't show every extreme that they name: `group_ids`: requests of one group stand in consecutive order; each of the 4 groups holds 1 to 16 requests and one holds exactly 16. Cache positions 0 to cache_len[g] - 1 of group g are live; one group's cache is full in every draw.
All inputs are finite; a program needn't handle non-finite values. No bound on the sum of `accept` on one device may be relied on, other than what follows from the above.
Results may differ from a plain program's by a relative error of at most 0.04.
Values may be sent and summed in bfloat16 or wider, within the bound.
A program may use at most 128 MiB of HBM per device.

v0:
```python
import jax
import jax.numpy as jnp
from jax import lax
from jax.sharding import PartitionSpec as P

PASSES = 2


def layer_norm(values):
    centre = values - jnp.mean(values, -1, keepdims=True)
    spread = jnp.mean(centre * centre, -1, keepdims=True)
    return centre * lax.rsqrt(spread + 1e-05)


def attend(projected, own_cache, lengths, head_dim):
    queries = projected[..., :head_dim]
    keys_new = projected[..., head_dim : 2 * head_dim]
    values_new = projected[..., 2 * head_dim :]
    factor = head_dim ** (-0.5)
    scores = (
        jnp.einsum("rqhd,rkhd->rhqk", queries, keys_new, preferred_element_type=jnp.float32)
        * factor
    )
    highest = jnp.max(scores, -1)
    weights_raw = jnp.exp(scores - highest[..., None])
    totals = jnp.sum(weights_raw, -1)
    gathered = jnp.einsum(
        "rhqk,rkhd->rhqd",
        weights_raw.astype(jnp.bfloat16),
        values_new,
        preferred_element_type=jnp.float32,
    )
    cache_size = own_cache.shape[1]
    key_span = min(1024, cache_size)

    def visit_block(block_index, carried):
        highest, totals, gathered = carried
        cache_piece = lax.dynamic_slice_in_dim(own_cache, block_index * key_span, key_span, 1)
        scores = (
            jnp.einsum(
                "rqhd,rkhd->rhqk",
                queries,
                cache_piece[..., :head_dim],
                preferred_element_type=jnp.float32,
            )
            * factor
        )
        position = block_index * key_span + jnp.arange(key_span, dtype=jnp.int32)
        scores = jnp.where(
            position[None, None, None, :] < lengths[:, None, None, None], scores, -1e30
        )
        raised = jnp.maximum(highest, jnp.max(scores, -1))
        shrink = jnp.exp(highest - raised)
        weights_raw = jnp.exp(scores - raised[..., None])
        totals = totals * shrink + jnp.sum(weights_raw, -1)
        gathered = gathered * shrink[..., None] + jnp.einsum(
            "rhqk,rkhd->rhqd",
            weights_raw.astype(jnp.bfloat16),
            cache_piece[..., head_dim:],
            preferred_element_type=jnp.float32,
        )
        return (raised, totals, gathered)

    highest, totals, gathered = lax.fori_loop(
        0, cache_size // key_span, visit_block, (highest, totals, gathered)
    )
    mixed_heads = gathered / totals[..., None]
    return jnp.transpose(mixed_heads, (0, 2, 1, 3)).astype(jnp.bfloat16)


def shards(
    tokens, cache_kv, w_qkv, w_out, w_fc, w_proj, embed_table, group_ids, cache_len, accept, new_ids
):
    req_index = lax.axis_index("req")
    per_device = tokens.shape[0]
    kv_width = cache_kv.shape[3]
    head_dim = kv_width // 2
    my_groups = lax.dynamic_slice_in_dim(group_ids, req_index * per_device, per_device)
    every_cache = lax.all_gather(cache_kv, "req", axis=1, tiled=True)
    own_cache = jnp.take(every_cache, my_groups, axis=0)
    lengths = jnp.take(cache_len, my_groups)
    vocab_dev = embed_table.shape[0]
    relative = new_ids - req_index * vocab_dev
    inside = (relative >= 0) & (relative < vocab_dev)
    looked = jnp.take(embed_table, jnp.clip(relative, 0, vocab_dev - 1), axis=0)
    looked = jnp.where(inside[..., None], looked, jnp.zeros((), jnp.bfloat16))
    picked = (
        lax.psum_scatter(looked, "req", scatter_dimension=1, tiled=True)
        .astype(jnp.float32)
        .astype(jnp.bfloat16)
    )
    fresh_rows = lax.all_gather(picked, "blk", axis=3, tiled=True)
    current = tokens
    for pass_index in range(PASSES):
        state_f32 = current.astype(jnp.float32)
        normed = layer_norm(state_f32).astype(jnp.bfloat16)
        projected = jnp.einsum(
            "rbd,dhc->rbhc", normed, w_qkv, preferred_element_type=jnp.float32
        ).astype(jnp.bfloat16)
        head_rows = attend(projected, own_cache, lengths, head_dim)
        partial_terms = jnp.einsum(
            "rbhc,hcd->rbd", head_rows, w_out, preferred_element_type=jnp.float32
        )
        middle = state_f32 + lax.psum(partial_terms.astype(jnp.bfloat16), "blk").astype(jnp.float32)
        normed_mid = layer_norm(middle).astype(jnp.bfloat16)
        hidden = jax.nn.gelu(
            jnp.einsum("rbd,df->rbf", normed_mid, w_fc, preferred_element_type=jnp.float32),
            approximate=True,
        ).astype(jnp.bfloat16)
        grown_rows = jnp.einsum("rbf,fd->rbd", hidden, w_proj, preferred_element_type=jnp.float32)
        current = (
            middle + lax.psum(grown_rows.astype(jnp.bfloat16), "blk").astype(jnp.float32)
        ).astype(jnp.bfloat16)
        current = jnp.where(accept[pass_index][..., None] == 1, fresh_rows[pass_index], current)
    return current


def solution(mesh):
    return jax.shard_map(
        shards,
        mesh=mesh,
        in_specs=(
            P("req", None, None),
            P(None, "req", "blk", None),
            P(None, "blk", None),
            P("blk", None, None),
            P(None, "blk"),
            P("blk", None),
            P("req", "blk"),
            P(),
            P(),
            P(None, "req", None),
            P(),
        ),
        out_specs=P("req", None, None),
        check_vma=False,
    )
```

profile of v0, /device:TPU:6, one launch (start us, length us, event | category | flops | bytes accessed | tf_op | source)
XLA Modules:
  0.0 969.9 jit_solution(16571325852743032627)
XLA Ops:
  9.8 57.4 %gather_fusion = bf16[16384,100]{1,0:T(8,128)(2,1)} fusion(bf16[3141,100]{1,0:T(8,128)(2,1)S(1)} %copy.29, s32[16384]{0:T(1024)S(1)} %broadcast_clamp_fusion), kind=kCustom, calls=%fused_computation | custom fusion | bytes 6619136 | tf_op jit(solution)/shard_map/jit(_take)/gather | solution.py:85
  67.2 7.7 copy.44
  74.9 2.3 select_select_fusion
  77.2 5.1 copy.31
  86.8 2.7 all-gather.5.cloned.1.call-done
  89.6 5.7 slice_bitcast_fusion.1
  95.3 4.4 gather_fusion.3
  99.6 4.3 gather_fusion.2
  103.9 4.0 maximum_select_fusion
  107.9 6.4 copy.37
  114.4 34.5 %while.34 = (s32[]{:T(128)}, f32[2,1,256]{2,0,1:T(2,128)S(1)}, f32[2,1,256]{2,0,1:T(2,128)S(1)}, f32[2,1,256,64]{2,3,0,1:T(8,128)S(1)}, s32[2]{0:T(128)S(1)}, /*...) while((s32[]{:T(128)}, f32[2,1,256]{2,0,1:T(2,128)S(1)}, ...), condition=%wide.region_8.9_spmd, body=%wide.region_5.8_spmd.sunk | while | flops 140055040 | bytes 7192775 | solution.py:64
  114.4 1.7 bitcast_reduce_fusion.4
  116.8 1.8 fusion.149
  121.1 1.8 fusion.149
  123.1 1.7 bitcast_reduce_fusion.4
  125.4 1.8 fusion.149
  129.7 1.8 fusion.149
  131.7 1.7 bitcast_reduce_fusion.4
  134.1 1.8 fusion.149
  138.4 1.8 fusion.149
  140.3 1.7 bitcast_reduce_fusion.4
  142.7 1.8 fusion.149
  144.7 1.7 bitcast_reduce_fusion.4
  147.0 1.8 fusion.149
  148.9 1.8 convolution_convert_fusion.1
  152.0 92.6 %all-reduce.15.cloned.1.call-done = bf16[2,32,256,100]{2,0,3,1:T(2,128)(2,1)} async-done(((bf16[2,32,256,100]{2,0,3,1:T(2,128)(2,1)}), bf16[2,32,256,100]{2,0,3,1:T(2,128)(2,1)}) %all-reduce.15.cloned.1.call-update) | async-done | bytes 3276816
  246.8 147.8 %all-reduce.7.cloned.1.call-done = bf16[2,256,1600]{1,2,0:T(8,128)(2,1)} async-done(((bf16[2,256,1600]{1,2,0:T(8,128)(2,1)}), bf16[2,256,1600]{1,2,0:T(8,128)(2,1)}) %all-reduce.7.cloned.1.call-update) | async-done | bytes 1638416 | tf_op jit(solution)/shard_map/psum | solution.py:104
  394.6 2.0 fusion.38
  397.3 5.1 convolution_convert_fusion.3
  402.5 75.9 %all-gather.3.cloned.1.call-done = bf16[2,2,256,1600]{2,1,0,3:T(2,128)(2,1)} async-done(((bf16[2,2,256,100]{2,1,0,3:T(2,128)(2,1)}), bf16[2,2,256,1600]{2,1,0,3:T(2,128)(2,1)}) %all-gather.3.cloned.1.call-update) | async-done | bytes 3276816 | tf_op jit(solution)/shard_map/all_gather | solution.py:92
  478.4 5.4 fusion.135
  483.8 139.8 %all-reduce.9.cloned.1.call-done = bf16[2,256,1600]{1,2,0:T(8,128)(2,1)} async-done(((bf16[2,256,1600]{1,2,0:T(8,128)(2,1)}), bf16[2,256,1600]{1,2,0:T(8,128)(2,1)}) %all-reduce.9.cloned.1.call-update) | async-done | bytes 1638416 | tf_op jit(solution)/shard_map/psum | solution.py:112
  623.6 3.4 convert_reduce_fusion
  628.8 34.4 %while.35 = (s32[]{:T(128)}, f32[2,1,256]{2,0,1:T(2,128)S(1)}, f32[2,1,256]{2,0,1:T(2,128)S(1)}, f32[2,1,256,64]{2,3,0,1:T(8,128)S(1)}, s32[2]{0:T(128)S(1)}, /*...) while((s32[]{:T(128)}, f32[2,1,256]{2,0,1:T(2,128)S(1)}, ...), condition=%wide.region_20.21_spmd, body=%wide.region_17.20_spmd.sunk | while | flops 140055040 | bytes 7192775 | solution.py:64
  631.3 1.8 fusion.153
  635.6 1.8 fusion.153
  639.9 1.8 fusion.153
  644.2 1.8 fusion.153
  648.5 1.8 fusion.153
  652.8 1.8 fusion.153
  657.1 1.8 fusion.153
  661.4 1.8 fusion.153
  663.3 1.8 convolution_convert_fusion
  665.4 142.6 %all-reduce.11.cloned.1.call-done = bf16[2,256,1600]{1,2,0:T(8,128)(2,1)} async-done(((bf16[2,256,1600]{1,2,0:T(8,128)(2,1)}), bf16[2,256,1600]{1,2,0:T(8,128)(2,1)}) %all-reduce.11.cloned.1.call-update) | async-done | bytes 1638416 | tf_op jit(solution)/shard_map/psum | solution.py:104
  808.0 2.0 fusion.39
  810.6 5.1 convolution_convert_fusion.2
  815.8 142.9 %all-reduce.13.cloned.1.call-done = bf16[2,256,1600]{1,2,0:T(8,128)(2,1)} async-done(((bf16[2,256,1600]{1,2,0:T(8,128)(2,1)}), bf16[2,256,1600]{1,2,0:T(8,128)(2,1)}) %all-reduce.13.cloned.1.call-update) | async-done | bytes 1638416 | tf_op jit(solution)/shard_map/psum | solution.py:112
  958.7 4.4 fusion.43
  (185 shorter events, 44.3 us)
Async XLA Ops:
  6.5 390.8 %copy-start = (bf16[400,1600]{1,0:T(8,128)(2,1)S(1)}, bf16[400,1600]{1,0:T(8,128)(2,1)}, u32[]{:S(2)}) copy-start(bf16[400,1600]{1,0:T(8,128)(2,1)} %param.20) | copy-start | bytes 3840004
  6.5 83.0 %all-gather.5.cloned.1.call-start = ((), (), s32[]{:S(2)}) async-start(), calls=%async_computation.1 | async-start | bytes 8912896 | tf_op jit(solution)/shard_map/all_gather | solution.py:79
  7.3 237.3 %all-reduce.15.cloned.1.call-start = ((), (), s32[]{:S(2)}) async-start(), calls=%async_computation.6 | async-start | bytes 6553600
  82.3 1.4 copy-start.2
  82.3 312.3 %all-reduce.7.cloned.1.call-start = ((), (), s32[]{:S(2)}) async-start(), calls=%async_computation.2 | async-start | bytes 3276800 | tf_op jit(solution)/shard_map/psum | solution.py:104
  83.7 1.1 copy-start.11
  84.8 1.3 copy-start.10
  84.8 1.4 copy-start.1
  85.5 9.8 %copy-start.7 = (bf16[2,256,1,192]{1,3,0,2:T(8,128)(2,1)}, bf16[2,256,1,192]{1,3,0,2:T(8,128)(2,1)S(1)}, u32[]{:S(2)}) copy-start(bf16[2,256,1,192]{1,3,0,2:T(8,128)(2,1)S(1)} %fusion.66) | copy-start | bytes 589828
  107.9 6.4 slice-start
  114.4 34.5 %copy-start.8 = (bf16[1,64,1600]{2,1,0:T(8,128)(2,1)S(1)}, bf16[1,64,1600]{2,1,0:T(8,128)(2,1)}, u32[]{:S(2)}) copy-start(bf16[1,64,1600]{2,1,0:T(8,128)(2,1)} %param.18) | copy-start | bytes 614404
  148.9 1.9 copy-start.13
  150.7 327.7 %all-gather.3.cloned.1.call-start = ((), (), s32[]{:S(2)}) async-start(), calls=%async_computation | async-start | bytes 3481600 | tf_op jit(solution)/shard_map/all_gather | solution.py:92
  246.6 377.0 %all-reduce.9.cloned.1.call-start = ((), (), s32[]{:S(2)}) async-start(), calls=%async_computation.3 | async-start | bytes 3276800 | tf_op jit(solution)/shard_map/psum | solution.py:112
  394.6 2.0 copy-start.5
  397.3 5.2 copy-start.9
  402.5 405.5 %all-reduce.11.cloned.1.call-start = ((), (), s32[]{:S(2)}) async-start(), calls=%async_computation.4 | async-start | bytes 3276800 | tf_op jit(solution)/shard_map/psum | solution.py:104
  623.6 3.9 copy-start.12
  627.0 1.2 copy-start.3
  663.2 144.7 %copy-start.4 = (bf16[2,256,1600]{1,2,0:T(8,128)(2,1)S(1)}, bf16[2,256,1600]{1,2,0:T(8,128)(2,1)}, u32[]{:S(2)}) copy-start(bf16[2,256,1600]{1,2,0:T(8,128)(2,1)} %copy-done.3) | copy-start | bytes 4915204
  665.1 293.6 %all-reduce.13.cloned.1.call-start = ((), (), s32[]{:S(2)}) async-start(), calls=%async_computation.5 | async-start | bytes 3276800 | tf_op jit(solution)/shard_map/psum | solution.py:112
  808.0 2.0 copy-start.6
Sparse Core Ops, SparseCore 0:
  10.1 79.3 all-gather.4
  92.2 152.3 all-reduce.14
  247.3 147.2 all-reduce.6
  396.4 81.9 all-gather.2
  481.1 142.4 all-reduce.8
  665.2 142.7 all-reduce.10
  815.9 142.7 all-reduce.12
where the time goes:
time: 971 us; the launch traced here: 970 us
  waiting for transfers between devices  745 us (77%)
  local copies, waits for them, and re-layouts  103 us (11%)
  matrix products  72.2 us (7%)
  other arithmetic  33.6 us (3%)
  between operations  14.4 us (1%)
    psum x2, waiting for transfers between devices, shards(): lax.psum(partial_terms.astype(jnp.bfloat16), 'blk').astype(jnp.float32)  290 us
    psum x2, waiting for transfers between devices, shards(): lax.psum(grown_rows.astype(jnp.bfloat16), 'blk').astype(jnp.float32)  283 us
    unnamed x8, waiting for transfers between devices  93.4 us
    all_gather x1, waiting for transfers between devices, shards(): fresh_rows = lax.all_gather(picked, 'blk', axis=3, tiled=True)  75.9 us
    gather x2, local copies, waits for them, and re-layouts, shards(): looked = jnp.take(embed_table, jnp.clip(relative, 0, vocab_dev - 1), axis=0)  65.1 us
    dot_general x16, matrix products, visit_block(): jnp.einsum('rhqk,rkhd->rhqd', weights_raw.astype(jnp.bfloat16), cache_pie...  29.2 us
    dot_general x16, matrix products, visit_block(): jnp.einsum('rqhd,rkhd->rhqk', queries, cache_piece[..., :head_dim], prefe...  26.9 us
  transfers between devices with their start and end apart: 7, of which 7 were waited for; matrix products, arithmetic and copies ran while one was open for 16% of the time, Pallas kernels for 0%

commit v1 on v0

--- a/solution.py
+++ b/solution.py
@@ -1,9 +1,17 @@
+import functools
 import jax
 import jax.numpy as jnp
 from jax import lax
 from jax.sharding import PartitionSpec as P
 
 PASSES = 2
+
+
+def _put_seats_all(m, link_axis):
+    return jnp.sum(jax.lax.all_gather(m, link_axis), axis=0)
+
+
+settle_seats_all = functools.partial(_put_seats_all, link_axis="blk")
 
 
 def layer_norm(values):
@@ -109,7 +117,7 @@
         ).astype(jnp.bfloat16)
         grown_rows = jnp.einsum("rbf,fd->rbd", hidden, w_proj, preferred_element_type=jnp.float32)
         current = (
-            middle + lax.psum(grown_rows.astype(jnp.bfloat16), "blk").astype(jnp.float32)
+            middle + settle_seats_all(grown_rows.astype(jnp.bfloat16)).astype(jnp.float32)
         ).astype(jnp.bfloat16)
         current = jnp.where(accept[pass_index][..., None] == 1, fresh_rows[pass_index], current)
     return current

time: 971 us -> 1800 us (1.85)
  waiting for transfers between devices: 745 us -> 1540 us
  other arithmetic: 33.6 us -> 62.8 us
    all_gather x0 -> x2, waiting for transfers between devices: none -> 1080 us  [_put_seats_all(): return jnp.sum(jax.lax.all_gather(m, link_axis), axis=0)]
    psum x2 -> x0, waiting for transfers between devices: 283 us -> none  [shards(): lax.psum(grown_rows.astype(jnp.bfloat16), 'blk').astype(jnp.float32)]
    reduce_sum x0 -> x2, other arithmetic: none -> 29.8 us  [_put_seats_all(): return jnp.sum(jax.lax.all_gather(m, link_axis), axis=0)]
  transfers between devices with their start and end apart: 7 -> 7, of which waited for: 7 -> 7; matrix products, arithmetic and copies ran while one was open for 16% -> 9% of each run, Pallas kernels for 0% -> 0%
where the time goes in v1:
time: 1800 us
  waiting for transfers between devices  1540 us (86%)
  local copies, waits for them, and re-layouts  102 us (6%)
  matrix products  83.5 us (5%)
  other arithmetic  62.8 us (3%)
    all_gather x2, waiting for transfers between devices, _put_seats_all(): return jnp.sum(jax.lax.all_gather(m, link_axis), axis=0)  1080 us
    psum x2, waiting for transfers between devices, shards(): lax.psum(partial_terms.astype(jnp.bfloat16), 'blk').astype(jnp.float32)  293 us
    unnamed x8, waiting for transfers between devices  90.1 us
    all_gather x1, waiting for transfers between devices, shards(): fresh_rows = lax.all_gather(picked, 'blk', axis=3, tiled=True)  75.9 us
    gather x2, local copies, waits for them, and re-layouts, shards(): looked = jnp.take(embed_table, jnp.clip(relative, 0, vocab_dev - 1), axis=0)  65.1 us
    dot_general x16, matrix products, visit_block(): jnp.einsum('rhqk,rkhd->rhqd', weights_raw.astype(jnp.bfloat16), cache_pie...  36.9 us
  transfers between devices with their start and end apart: 7, of which 7 were waited for; matrix products, arithmetic and copies ran while one was open for 9% of the time, Pallas kernels for 0%

profile of v1, /device:TPU:6, one launch (start us, length us, event | category | flops | bytes accessed | tf_op | source)
XLA Modules:
  0.0 1799.7 jit_solution(6120267539857099011)
XLA Ops:
  9.8 57.4 %gather_fusion = bf16[16384,100]{1,0:T(8,128)(2,1)} fusion(bf16[3141,100]{1,0:T(8,128)(2,1)S(1)} %copy.29, s32[16384]{0:T(1024)S(1)} %broadcast_clamp_fusion), kind=kCustom, calls=%fused_computation | custom fusion | bytes 6619136 | tf_op jit(solution)/shard_map/jit(_take)/gather | solution.py:93
  67.2 7.7 copy.44
  74.9 2.3 select_select_fusion
  77.2 5.1 copy.31
  87.5 2.1 all-gather.9.cloned.1.call-done
  89.6 5.7 slice_bitcast_fusion.1
  95.3 3.1 gather_fusion.2
  98.4 4.3 gather_fusion.3
  102.8 3.7 maximum_select_fusion
  106.4 6.4 copy.37
  112.9 38.1 %while.34 = (s32[]{:T(128)}, f32[2,1,256]{2,0,1:T(2,128)S(1)}, f32[2,1,256]{2,0,1:T(2,128)S(1)}, f32[2,1,256,64]{2,3,0,1:T(8,128)}, s32[2]{0:T(128)S(1)}, /*inde...) while((s32[]{:T(128)}, f32[2,1,256]{2,0,1:T(2,128)S(1)}, ...), condition=%wide.region_8.9_spmd, body=%wide.region_5.8_spmd.sunk | while | flops 140055040 | bytes 7192775 | solution.py:72
  112.9 1.7 bitcast_reduce_fusion.4
  114.6 2.3 fusion.149
  119.4 2.3 fusion.149
  122.5 1.7 bitcast_reduce_fusion.4
  124.2 2.3 fusion.149
  128.9 2.3 fusion.149
  132.0 1.7 bitcast_reduce_fusion.4
  133.7 2.3 fusion.149
  138.5 2.3 fusion.149
  143.2 2.3 fusion.149
  148.0 2.3 fusion.149
  151.0 2.9 convolution_convert_fusion.1
  155.3 89.3 %all-reduce.9.cloned.1.call-done = bf16[2,32,256,100]{2,0,3,1:T(2,128)(2,1)} async-done(((bf16[2,32,256,100]{2,0,3,1:T(2,128)(2,1)}), bf16[2,32,256,100]{2,0,3,1:T(2,128)(2,1)}) %all-reduce.9.cloned.1.call-update) | async-done | bytes 3276816
  246.7 147.8 %all-reduce.5.cloned.1.call-done = bf16[2,256,1600]{1,2,0:T(8,128)(2,1)} async-done(((bf16[2,256,1600]{1,2,0:T(8,128)(2,1)}), bf16[2,256,1600]{1,2,0:T(8,128)(2,1)}) %all-reduce.5.cloned.1.call-update) | async-done | bytes 1638416 | tf_op jit(solution)/shard_map/psum | solution.py:112
  394.5 2.0 fusion.38
  397.3 5.1 convolution_convert_fusion.3
  402.5 75.9 %all-gather.7.cloned.1.call-done = bf16[2,2,256,1600]{2,1,0,3:T(2,128)(2,1)} async-done(((bf16[2,2,256,100]{2,1,0,3:T(2,128)(2,1)}), bf16[2,2,256,1600]{2,1,0,3:T(2,128)(2,1)}) %all-gather.7.cloned.1.call-update) | async-done | bytes 3276816 | tf_op jit(solution)/shard_map/all_gather | solution.py:100
  478.4 5.3 fusion.135
  483.7 535.7 %all-gather.11.cloned.1.call-done = bf16[32,256,1600]{1,2,0:T(8,128)(2,1)} async-done(((bf16[2,256,1600]{1,2,0:T(8,128)(2,1)}), bf16[32,256,1600]{1,2,0:T(8,128)(2,1)}) %all-gather.11.cloned.1.call-update) | async-done | bytes 26214416 | tf_op jit(solution)/shard_map/all_gather | solution.py:11
  1019.4 14.9 reduce_sum.150
  1034.4 3.4 convert_reduce_fusion
  1040.2 38.1 %while.35 = (s32[]{:T(128)}, f32[2,1,256]{2,0,1:T(2,128)S(1)}, f32[2,1,256]{2,0,1:T(2,128)S(1)}, f32[2,1,256,64]{2,3,0,1:T(8,128)}, s32[2]{0:T(128)S(1)}, /*inde...) while((s32[]{:T(128)}, f32[2,1,256]{2,0,1:T(2,128)S(1)}, ...), condition=%wide.region_20.21_spmd, body=%wide.region_17.20_spmd.sunk | while | flops 140055040 | bytes 7192775 | solution.py:72
  1042.0 2.3 fusion.153
  1046.8 2.3 fusion.153
  1051.5 2.3 fusion.153
  1056.3 2.3 fusion.153
  1061.1 2.3 fusion.153
  1065.8 2.3 fusion.153
  1070.6 2.3 fusion.153
  1075.4 2.3 fusion.153
  1078.3 2.9 convolution_convert_fusion
  1081.6 144.8 %all-reduce.7.cloned.1.call-done = bf16[2,256,1600]{1,2,0:T(8,128)(2,1)} async-done(((bf16[2,256,1600]{1,2,0:T(8,128)(2,1)}), bf16[2,256,1600]{1,2,0:T(8,128)(2,1)}) %all-reduce.7.cloned.1.call-update) | async-done | bytes 1638416 | tf_op jit(solution)/shard_map/psum | solution.py:112
  1226.3 2.0 fusion.39
  1229.0 5.1 convolution_convert_fusion.2
  1234.1 539.4 %all-gather.13.cloned.1.call-done = bf16[32,256,1600]{1,2,0:T(8,128)(2,1)} async-done(((bf16[2,256,1600]{1,2,0:T(8,128)(2,1)}), bf16[32,256,1600]{1,2,0:T(8,128)(2,1)}) %all-gather.13.cloned.1.call-update) | async-done | bytes 26214416 | tf_op jit(solution)/shard_map/all_gather | solution.py:11
  1773.5 14.9 reduce_sum.157
  1788.5 4.4 fusion.43
  (187 shorter events, 48.7 us)
Async XLA Ops:
  6.5 390.7 %copy-start = (bf16[400,1600]{1,0:T(8,128)(2,1)S(1)}, bf16[400,1600]{1,0:T(8,128)(2,1)}, u32[]{:S(2)}) copy-start(bf16[400,1600]{1,0:T(8,128)(2,1)} %param.20) | copy-start | bytes 3840004
  6.5 83.0 %all-gather.9.cloned.1.call-start = ((), (), s32[]{:S(2)}) async-start(), calls=%async_computation.1 | async-start | bytes 8912896 | tf_op jit(solution)/shard_map/all_gather | solution.py:87
  7.3 237.3 %all-reduce.9.cloned.1.call-start = ((), (), s32[]{:S(2)}) async-start(), calls=%async_computation.6 | async-start | bytes 6553600
  82.3 1.4 copy-start.2
  82.3 312.2 %all-reduce.5.cloned.1.call-start = ((), (), s32[]{:S(2)}) async-start(), calls=%async_computation.2 | async-start | bytes 3276800 | tf_op jit(solution)/shard_map/psum | solution.py:112
  83.7 1.1 copy-start.11
  84.8 1.9 copy-start.10
  84.8 2.0 copy-start.1
  85.4 1.3 copy-start.8
  106.4 6.4 slice-start
  151.0 3.0 copy-start.13
  151.0 243.6 %copy-start.3 = (bf16[2,256,1600]{1,2,0:T(8,128)(2,1)S(1)}, bf16[2,256,1600]{1,2,0:T(8,128)(2,1)}, u32[]{:S(2)}) copy-start(bf16[2,256,1600]{1,2,0:T(8,128)(2,1)} %param.15) | copy-start | bytes 4915204
  153.9 324.4 %all-gather.7.cloned.1.call-start = ((), (), s32[]{:S(2)}) async-start(), calls=%async_computation | async-start | bytes 3481600 | tf_op jit(solution)/shard_map/all_gather | solution.py:100
  246.5 773.0 %all-gather.11.cloned.1.call-start = ((), (), s32[]{:S(2)}) async-start(), calls=%async_computation.4 | async-start | bytes 27852800 | tf_op jit(solution)/shard_map/all_gather | solution.py:11
  394.5 2.0 copy-start.6
  397.2 5.2 copy-start.9
  402.4 823.9 %all-reduce.7.cloned.1.call-start = ((), (), s32[]{:S(2)}) async-start(), calls=%async_computation.3 | async-start | bytes 3276800 | tf_op jit(solution)/shard_map/psum | solution.py:112
  1034.4 3.9 copy-start.12
  1037.8 1.2 copy-start.4
  1078.3 148.0 %copy-start.5 = (bf16[2,256,1600]{1,2,0:T(8,128)(2,1)S(1)}, bf16[2,256,1600]{1,2,0:T(8,128)(2,1)}, u32[]{:S(2)}) copy-start(bf16[2,256,1600]{1,2,0:T(8,128)(2,1)} %copy-done.4) | copy-start | bytes 4915204
  1081.3 692.3 %all-gather.13.cloned.1.call-start = ((), (), s32[]{:S(2)}) async-start(), calls=%async_computation.5 | async-start | bytes 27852800 | tf_op jit(solution)/shard_map/all_gather | solution.py:11
  1226.3 2.0 copy-start.7
Sparse Core Ops, SparseCore 0:
  10.1 79.3 all-gather.8
  92.2 152.2 all-reduce.8
  247.2 147.2 all-reduce.4
  396.3 81.9 all-gather.6
  480.1 539.2 all-gather.10
  1081.4 144.8 all-reduce.6
  1234.3 539.2 all-gather.12
